TPU v7x, 32 devices: a whole 2x2x4 slice. The times are simulated.
32 devices in a mesh: dp: 8 (over z, y), tensor: 4 (over x, core).
Axes of the slice: x: 2, y: 2, z: 4, core: 2. Of those that a mesh axis runs over, the one named last changes fastest.
Arguments:
- tokens: bfloat16 [32768, 768], P(('dp', 'tensor')), may hold values from -6 to 6
- doc_lengths: int32 [32, 16], P('dp'), may hold values from 1 to 512, 1024 in all within a row
- w_query: bfloat16 [768, 768], P('dp', 'tensor'), may hold values from -0.21875 to 0.21875
- w_key: bfloat16 [768, 768], P('dp', 'tensor'), may hold values from -0.21875 to 0.21875
- w_value: bfloat16 [768, 768], P('dp', 'tensor'), may hold values from -0.21875 to 0.21875
- w_out: bfloat16 [768, 768], P('tensor', 'dp'), may hold values from -1.25 to 1.25
- w_up: bfloat16 [768, 3072], P('dp', 'tensor'), may hold values from -0.21875 to 0.21875
- w_down: bfloat16 [3072, 768], P('tensor', 'dp'), may hold values from -0.109375 to 0.109375
- b_query: bfloat16 [12, 64], P('tensor', 'dp'), may hold values from -3 to 3
- b_value: bfloat16 [12, 64], P('tensor', 'dp'), may hold values from -3 to 3
- b_up: bfloat16 [24, 128], P('tensor', 'dp'), may hold values from -3 to 3
- b_out: float32 [768], P(('dp', 'tensor')), may hold values from -3 to 3
- b_down: float32 [768], P(('dp', 'tensor')), may hold values from -3 to 3
- gain_one: float32 [768], P(('dp', 'tensor')), may hold values from 0.1 to 1.9
- shift_one: float32 [768], P(('dp', 'tensor')), may hold values from -3 to 3
- gain_two: float32 [768], P(('dp', 'tensor')), may hold values from 0.1 to 1.9
- shift_two: float32 [768], P(('dp', 'tensor')), may hold values from -3 to 3
- cotangent: bfloat16 [32768, 768], P(('dp', 'tensor')), may hold values from -6 to 6
Outputs:
- layer_out: bfloat16 [32768, 768], P(('dp', 'tensor'))
- grad_tokens: bfloat16 [32768, 768], P(('dp', 'tensor'))
- grad_w_query: float32 [768, 768], P('dp', 'tensor')
- grad_w_key: float32 [768, 768], P('dp', 'tensor')
- grad_w_value: float32 [768, 768], P('dp', 'tensor')
- grad_w_out: float32 [768, 768], P('tensor', 'dp')
- grad_w_up: float32 [768, 3072], P('dp', 'tensor')
- grad_w_down: float32 [3072, 768], P('tensor', 'dp')
- grad_b_query: float32 [12, 64], P('tensor', 'dp')
- grad_b_value: float32 [12, 64], P('tensor', 'dp')
- grad_b_up: float32 [24, 128], P('tensor', 'dp')
- grad_b_out: float32 [768], P(('dp', 'tensor'))
- grad_b_down: float32 [768], P(('dp', 'tensor'))
- grad_gain_one: float32 [768], P(('dp', 'tensor'))
- grad_shift_one: float32 [768], P(('dp', 'tensor'))
- grad_gain_two: float32 [768], P(('dp', 'tensor'))
- grad_shift_two: float32 [768], P(('dp', 'tensor'))
Inputs may be any that keep to these rules, and one draw needn't show every extreme that they name: `doc_lengths`: each row holds the 16 document lengths of one sequence in order and sums to 1024.
All inputs are finite; a program needn't handle non-finite values.
Results may differ from a plain program's by a relative error of at most 0.02.
Values may be sent and summed in bfloat16 or wider, within the bound.
No kernel may reach another device: no remote copies, remote signals or barrier semaphores. Data moves between devices by JAX's collectives and lax.ppermute only.
A program may use at most 192 MiB of HBM per device.

v0:
```python
import jax
import jax.numpy as jnp
from jax import lax
from jax.sharding import PartitionSpec as P

HD = 64
LEN = 1024
epsilon = 1e-06
root_half = 0.7071067811865476
inv_root_tau = 0.3989422804014327
masked_value = -1e30


def normalize(values, norm_gain, norm_shift):
    average = jnp.mean(values, axis=-1, keepdims=True)
    centred = values - average
    variance = jnp.mean(centred * centred, axis=-1, keepdims=True)
    inv_scale = lax.rsqrt(variance + epsilon)
    unit_rows = centred * inv_scale
    return (unit_rows * norm_gain + norm_shift, unit_rows, inv_scale)


def normalize_back(grad_out, unit_rows, inv_scale, norm_gain):
    grad_unit = grad_out * norm_gain
    middle = grad_unit - jnp.mean(grad_unit, axis=-1, keepdims=True)
    middle = middle - unit_rows * jnp.mean(grad_unit * unit_rows, axis=-1, keepdims=True)
    return inv_scale * middle


def gelu_parts(up_pre):
    normal_cdf = 0.5 * (1.0 + lax.erf(up_pre * root_half))
    return (
        up_pre * normal_cdf,
        normal_cdf + up_pre * inv_root_tau * jnp.exp(-0.5 * up_pre * up_pre),
    )


def segment_ids(doc_lengths, length):
    bounds = jnp.cumsum(doc_lengths, axis=-1)
    places = lax.broadcasted_iota(jnp.int32, (1, length, 1), 1)
    return jnp.sum((bounds[:, None, :] <= places).astype(jnp.int32), axis=-1)


def block_scores(query_block, key_seq, seg_block, seg_seq):
    scale = query_block.shape[-1] ** (-0.5)
    scores = (
        jnp.einsum("qhd,khd->hqk", query_block, key_seq, preferred_element_type=jnp.float32) * scale
    )
    allowed = seg_block[:, None] == seg_seq[None, :]
    return jnp.where(allowed[None], scores, masked_value)


def attention_forward(queries, keys_all, values_all, segments):
    seq_count, length = segments.shape
    head_count = queries.shape[1] // HD
    block_rows = min(512, length)
    shaped = (seq_count, length, head_count, HD)

    def one_sequence(inputs):
        query_one, key_one, value_one, seg_one = inputs
        outputs = []
        totals = []
        for offset in range(0, length, block_rows):
            ending = offset + block_rows
            scores = block_scores(
                query_one[offset:ending], key_one, seg_one[offset:ending], seg_one
            )
            row_top = jnp.max(scores, axis=-1, keepdims=True)
            weights = jnp.exp(scores - row_top)
            row_total = jnp.sum(weights, axis=-1, keepdims=True)
            probability = (weights / row_total).astype(jnp.bfloat16)
            mixture = jnp.einsum(
                "hqk,khd->qhd", probability, value_one, preferred_element_type=jnp.float32
            )
            outputs.append(mixture.astype(jnp.bfloat16))
            totals.append(row_top[..., 0] + jnp.log(row_total[..., 0]))
        return (jnp.concatenate(outputs, axis=0), jnp.concatenate(totals, axis=1))

    mixture, log_totals = lax.map(
        one_sequence,
        (queries.reshape(shaped), keys_all.reshape(shaped), values_all.reshape(shaped), segments),
    )
    return (mixture.reshape(seq_count * length, head_count * HD), log_totals)


def attention_backward(queries, keys_all, values_all, segments, log_totals, grad_mixture):
    seq_count, length = segments.shape
    head_count = queries.shape[1] // HD
    block_rows = min(512, length)
    shaped = (seq_count, length, head_count, HD)
    scale = HD ** (-0.5)

    def one_sequence(inputs):
        query_one, key_one, value_one, seg_one, grad_one, total_one = inputs
        grad_keys = jnp.zeros(key_one.shape, jnp.float32)
        grad_values = jnp.zeros(value_one.shape, jnp.float32)
        grad_queries = []
        for offset in range(0, length, block_rows):
            ending = offset + block_rows
            scores = block_scores(
                query_one[offset:ending], key_one, seg_one[offset:ending], seg_one
            )
            probability = jnp.exp(scores - total_one[:, offset:ending, None])
            grad_block = grad_one[offset:ending]
            grad_prob = jnp.einsum(
                "qhd,khd->hqk", grad_block, value_one, preferred_element_type=jnp.float32
            )
            inner = jnp.sum(probability * grad_prob, axis=-1, keepdims=True)
            grad_scores = (probability * (grad_prob - inner)).astype(jnp.bfloat16)
            block_query = jnp.einsum(
                "hqk,khd->qhd", grad_scores, key_one, preferred_element_type=jnp.float32
            )
            grad_queries.append((block_query * scale).astype(jnp.bfloat16))
            grad_keys = (
                grad_keys
                + jnp.einsum(
                    "hqk,qhd->khd",
                    grad_scores,
                    query_one[offset:ending],
                    preferred_element_type=jnp.float32,
                )
                * scale
            )
            grad_values = grad_values + jnp.einsum(
                "hqk,qhd->khd",
                probability.astype(jnp.bfloat16),
                grad_block,
                preferred_element_type=jnp.float32,
            )
        return (
            jnp.concatenate(grad_queries, axis=0),
            grad_keys.astype(jnp.bfloat16),
            grad_values.astype(jnp.bfloat16),
        )

    grad_q, grad_k, grad_v = lax.map(
        one_sequence,
        (
            queries.reshape(shaped),
            keys_all.reshape(shaped),
            values_all.reshape(shaped),
            segments,
            grad_mixture.reshape(shaped),
            log_totals,
        ),
    )
    flat = (seq_count * length, head_count * HD)
    return (grad_q.reshape(flat), grad_k.reshape(flat), grad_v.reshape(flat))


def per_device(
    tokens,
    doc_lengths,
    w_query,
    w_key,
    w_value,
    w_out,
    w_up,
    w_down,
    b_query,
    b_value,
    b_up,
    b_out,
    b_down,
    gain_one,
    shift_one,
    gain_two,
    shift_two,
    cotangent,
):
    segments = segment_ids(doc_lengths, LEN)
    gathered = (
        lax.all_gather(w_query, "dp", axis=0, tiled=True),
        lax.all_gather(w_key, "dp", axis=0, tiled=True),
        lax.all_gather(w_value, "dp", axis=0, tiled=True),
        lax.all_gather(w_out, "dp", axis=1, tiled=True),
        lax.all_gather(w_up, "dp", axis=0, tiled=True),
        lax.all_gather(w_down, "dp", axis=1, tiled=True),
        lax.all_gather(b_query, "dp", axis=1, tiled=True),
        lax.all_gather(b_value, "dp", axis=1, tiled=True),
        lax.all_gather(b_up, "dp", axis=1, tiled=True),
    )
    (
        full_query,
        full_key,
        full_value,
        full_out,
        full_up,
        full_down,
        bias_query,
        bias_value,
        bias_up,
    ) = gathered
    vectors = (
        lax.all_gather(b_out, ("dp", "tensor"), axis=0, tiled=True),
        lax.all_gather(b_down, ("dp", "tensor"), axis=0, tiled=True),
        lax.all_gather(gain_one, ("dp", "tensor"), axis=0, tiled=True),
        lax.all_gather(shift_one, ("dp", "tensor"), axis=0, tiled=True),
        lax.all_gather(gain_two, ("dp", "tensor"), axis=0, tiled=True),
        lax.all_gather(shift_two, ("dp", "tensor"), axis=0, tiled=True),
    )
    bias_out, bias_down, norm_gain_one, norm_shift_one, norm_gain_two, norm_shift_two = vectors
    local_rows = tokens.shape[0]
    tokens_all = lax.all_gather(tokens, "tensor", axis=0, tiled=True)
    queries = (
        jnp.dot(tokens_all, full_query, preferred_element_type=jnp.float32)
        + bias_query.reshape(-1).astype(jnp.float32)
    ).astype(jnp.bfloat16)
    keys_all = jnp.dot(tokens_all, full_key, preferred_element_type=jnp.float32).astype(
        jnp.bfloat16
    )
    values_all = (
        jnp.dot(tokens_all, full_value, preferred_element_type=jnp.float32)
        + bias_value.reshape(-1).astype(jnp.float32)
    ).astype(jnp.bfloat16)
    mixture, log_totals = attention_forward(queries, keys_all, values_all, segments)
    piece = lax.slice_in_dim(mixture, 0, local_rows * lax.axis_size("tensor"), axis=0)
    attn_part = lax.psum_scatter(
        jnp.dot(piece, full_out, preferred_element_type=jnp.float32).astype(jnp.bfloat16),
        "tensor",
        scatter_dimension=0,
        tiled=True,
    ).astype(jnp.float32)
    residual_one = attn_part + bias_out + tokens.astype(jnp.float32)
    first, unit_one, scale_one = normalize(residual_one, norm_gain_one, norm_shift_one)
    first_all = lax.all_gather(first.astype(jnp.bfloat16), "tensor", axis=0, tiled=True)
    up_pre = jnp.dot(first_all, full_up, preferred_element_type=jnp.float32) + bias_up.reshape(
        -1
    ).astype(jnp.float32)
    activated, slope = gelu_parts(up_pre)
    activated = activated.astype(jnp.bfloat16)
    piece = lax.slice_in_dim(activated, 0, local_rows * lax.axis_size("tensor"), axis=0)
    ffn_part = lax.psum_scatter(
        jnp.dot(piece, full_down, preferred_element_type=jnp.float32).astype(jnp.bfloat16),
        "tensor",
        scatter_dimension=0,
        tiled=True,
    ).astype(jnp.float32)
    residual_two = ffn_part + bias_down + first
    result, unit_two, scale_two = normalize(residual_two, norm_gain_two, norm_shift_two)
    grad_out = cotangent.astype(jnp.float32)
    grad_two = normalize_back(grad_out, unit_two, scale_two, norm_gain_two)
    grad_gain_two = jnp.sum(grad_out * unit_two, axis=0)
    grad_shift_two = jnp.sum(grad_out, axis=0)
    grad_bias_down = jnp.sum(grad_two, axis=0)
    grad_two_all = lax.all_gather(grad_two.astype(jnp.bfloat16), "tensor", axis=0, tiled=True)
    grad_w_down = jnp.einsum(
        "tf,td->fd", activated, grad_two_all, preferred_element_type=jnp.float32
    )
    grad_active = jnp.einsum(
        "td,fd->tf", grad_two_all, full_down, preferred_element_type=jnp.float32
    )
    grad_up = (grad_active * slope).astype(jnp.bfloat16)
    grad_bias_up = jnp.sum(grad_up, axis=0, dtype=jnp.float32)
    grad_w_up = jnp.einsum("td,tf->df", first_all, grad_up, preferred_element_type=jnp.float32)
    piece = lax.slice_in_dim(grad_up, 0, local_rows * lax.axis_size("tensor"), axis=0)
    grad_first = (
        lax.psum_scatter(
            jnp.einsum("tf,df->td", piece, full_up, preferred_element_type=jnp.float32).astype(
                jnp.bfloat16
            ),
            "tensor",
            scatter_dimension=0,
            tiled=True,
        ).astype(jnp.float32)
        + grad_two
    )
    grad_one = normalize_back(grad_first, unit_one, scale_one, norm_gain_one)
    grad_gain_one = jnp.sum(grad_first * unit_one, axis=0)
    grad_shift_one = jnp.sum(grad_first, axis=0)
    grad_bias_out = jnp.sum(grad_one, axis=0)
    grad_one_all = lax.all_gather(grad_one.astype(jnp.bfloat16), "tensor", axis=0, tiled=True)
    grad_w_out = jnp.einsum("th,td->hd", mixture, grad_one_all, preferred_element_type=jnp.float32)
    grad_mixture = jnp.einsum(
        "td,hd->th", grad_one_all, full_out, preferred_element_type=jnp.float32
    ).astype(jnp.bfloat16)
    grad_queries, grad_keys, grad_values = attention_backward(
        queries, keys_all, values_all, segments, log_totals, grad_mixture
    )
    grad_bias_query = jnp.sum(grad_queries, axis=0, dtype=jnp.float32)
    grad_bias_value = jnp.sum(grad_values, axis=0, dtype=jnp.float32)
    grad_w_query = jnp.einsum(
        "td,th->dh", tokens_all, grad_queries, preferred_element_type=jnp.float32
    )
    grad_w_key = jnp.einsum("td,th->dh", tokens_all, grad_keys, preferred_element_type=jnp.float32)
    grad_w_value = jnp.einsum(
        "td,th->dh", tokens_all, grad_values, preferred_element_type=jnp.float32
    )
    part_query = lax.slice_in_dim(grad_queries, 0, local_rows * lax.axis_size("tensor"), axis=0)
    part_key = lax.slice_in_dim(grad_keys, 0, local_rows * lax.axis_size("tensor"), axis=0)
    part_value = lax.slice_in_dim(grad_values, 0, local_rows * lax.axis_size("tensor"), axis=0)
    summed = jnp.einsum("th,dh->td", part_query, full_query, preferred_element_type=jnp.float32)
    summed = summed + jnp.einsum(
        "th,dh->td", part_key, full_key, preferred_element_type=jnp.float32
    )
    grad_input = (
        lax.psum_scatter(
            (
                summed
                + jnp.einsum(
                    "th,dh->td", part_value, full_value, preferred_element_type=jnp.float32
                )
            ).astype(jnp.bfloat16),
            "tensor",
            scatter_dimension=0,
            tiled=True,
        ).astype(jnp.float32)
        + grad_one
    )
    sent = (
        lax.psum_scatter(grad_w_query, "dp", scatter_dimension=0, tiled=True),
        lax.psum_scatter(grad_w_key, "dp", scatter_dimension=0, tiled=True),
        lax.psum_scatter(grad_w_value, "dp", scatter_dimension=0, tiled=True),
        lax.psum_scatter(grad_w_out, "dp", scatter_dimension=1, tiled=True),
        lax.psum_scatter(grad_w_up, "dp", scatter_dimension=0, tiled=True),
        lax.psum_scatter(grad_w_down, "dp", scatter_dimension=1, tiled=True),
        lax.psum_scatter(grad_bias_query.reshape(-1, HD), "dp", scatter_dimension=1, tiled=True),
        lax.psum_scatter(grad_bias_value.reshape(-1, HD), "dp", scatter_dimension=1, tiled=True),
        lax.psum_scatter(grad_bias_up.reshape(-1, 128), "dp", scatter_dimension=1, tiled=True),
    )
    vector_sums = (
        lax.psum_scatter(grad_bias_out, ("dp", "tensor"), scatter_dimension=0, tiled=True),
        lax.psum_scatter(grad_bias_down, ("dp", "tensor"), scatter_dimension=0, tiled=True),
        lax.psum_scatter(grad_gain_one, ("dp", "tensor"), scatter_dimension=0, tiled=True),
        lax.psum_scatter(grad_shift_one, ("dp", "tensor"), scatter_dimension=0, tiled=True),
        lax.psum_scatter(grad_gain_two, ("dp", "tensor"), scatter_dimension=0, tiled=True),
        lax.psum_scatter(grad_shift_two, ("dp", "tensor"), scatter_dimension=0, tiled=True),
    )
    return (
        result.astype(jnp.bfloat16),
        grad_input.astype(jnp.bfloat16),
        sent[0],
        sent[1],
        sent[2],
        sent[3],
        sent[4],
        sent[5],
        sent[6],
        sent[7],
        sent[8],
        vector_sums[0],
        vector_sums[1],
        vector_sums[2],
        vector_sums[3],
        vector_sums[4],
        vector_sums[5],
    )


def solution(mesh):
    placed = (
        P(("dp", "tensor"), None),
        P("dp", None),
        P("dp", "tensor"),
        P("dp", "tensor"),
        P("dp", "tensor"),
        P("tensor", "dp"),
        P("dp", "tensor"),
        P("tensor", "dp"),
        P("tensor", "dp"),
        P("tensor", "dp"),
        P("tensor", "dp"),
        P(("dp", "tensor")),
        P(("dp", "tensor")),
        P(("dp", "tensor")),
        P(("dp", "tensor")),
        P(("dp", "tensor")),
        P(("dp", "tensor")),
        P(("dp", "tensor"), None),
    )
    return jax.shard_map(
        per_device,
        mesh=mesh,
        in_specs=placed,
        out_specs=(
            P(("dp", "tensor"), None),
            P(("dp", "tensor"), None),
            P("dp", "tensor"),
            P("dp", "tensor"),
            P("dp", "tensor"),
            P("tensor", "dp"),
            P("dp", "tensor"),
            P("tensor", "dp"),
            P("tensor", "dp"),
            P("tensor", "dp"),
            P("tensor", "dp"),
            P(("dp", "tensor")),
            P(("dp", "tensor")),
            P(("dp", "tensor")),
            P(("dp", "tensor")),
            P(("dp", "tensor")),
            P(("dp", "tensor")),
        ),
        check_vma=False,
    )
```

profile of v0, /device:TPU:0, one launch (start us, length us, event | category | flops | bytes accessed | tf_op | source)
XLA Modules:
  0.0 1349.3 jit_solution(8543374420555080612)
XLA Ops:
  9.7 22.5 %all-gather.1 = bf16[8,8,3]{1,2,0:T(4,128)(2,1)S(1)} all-gather(bf16[1,8,3]{1,2,0:T(4,128)(2,1)} %bitcast.319), channel_id=1, replica_groups=mesh['dp'=8,'tensor'=4] {'dp'}, dimensions={0}, use_global_device_ids=true | all-gather | bytes 432 | tf_op jit(solution)/shard_map/all_gather | solution.py:179
  32.9 16.6 %all-gather = bf16[8,8,3]{1,2,0:T(4,128)(2,1)S(1)} all-gather(bf16[1,8,3]{1,2,0:T(4,128)(2,1)} %bitcast.320), channel_id=1, replica_groups=mesh['dp'=8,'tensor'=4] {'dp'}, dimensions={0}, use_global_device_ids=true | all-gather | bytes 432 | tf_op jit(solution)/shard_map/all_gather | solution.py:180
  50.7 31.2 %all_gather.63 = bf16[192,768]{0,1:T(8,128)(2,1)S(1)} all-gather(bf16[192,96]{0,1:T(8,128)(2,1)S(1)} %copy.104), channel_id=1, replica_groups=mesh['dp'=8,'tensor'=4] {'dp'}, dimensions={1}, use_global_device_ids=true | all-gather | bytes 331776 | tf_op jit(solution)/shard_map/all_gather | solution.py:176
  81.9 33.3 %all_gather.60 = bf16[768,192]{1,0:T(8,128)(2,1)} all-gather(bf16[96,192]{1,0:T(8,128)(2,1)} %param.24), channel_id=1, replica_groups=mesh['dp'=8,'tensor'=4] {'dp'}, dimensions={0}, use_global_device_ids=true | all-gather | bytes 331776 | tf_op jit(solution)/shard_map/all_gather | solution.py:173
  115.2 33.3 %all_gather.62 = bf16[768,192]{1,0:T(8,128)(2,1)} all-gather(bf16[96,192]{1,0:T(8,128)(2,1)} %param.25), channel_id=1, replica_groups=mesh['dp'=8,'tensor'=4] {'dp'}, dimensions={0}, use_global_device_ids=true | all-gather | bytes 331776 | tf_op jit(solution)/shard_map/all_gather | solution.py:174
  148.6 31.0 %all_gather.58 = bf16[768,192]{1,0:T(8,128)(2,1)S(1)} all-gather(bf16[96,192]{1,0:T(8,128)(2,1)S(1)} %copy-done.38), channel_id=1, replica_groups=mesh['dp'=8,'tensor'=4] {'dp'}, dimensions={0}, use_global_device_ids=true | all-gather | bytes 331776 | tf_op jit(solution)/shard_map/all_gather | solution.py:175
  205.9 52.6 %while.26 = (s32[]{:T(128)}, bf16[4,1024,3,64]{1,3,2,0:T(8,128)(2,1)}, f32[4,3,1024]{2,1,0:T(4,128)}, bf16[4,1024,3,64]{1,3,2,0:T(8,128)(2,1)}, s32[4,1024]{1,0:...) while((s32[]{:T(128)}, ...), condition=%wide.region_7.8_spmd, body=%wide.region_2.7_spmd.sunk | while | flops 845086720 | bytes 51542704 | solution.py:79
  278.5 39.3 %all-reduce.15 = (f32[768]{0:T(1024)}, f32[768]{0:T(1024)}, f32[768]{0:T(1024)}, f32[768]{0:T(1024)}, f32[768]{0:T(1024)}) all-reduce(f32[768]{0:T(1024)} %dynamic-update-slice.2, f32[768]{0:T(1024)} %dynamic-update-slice.1, f32[768]{0:T(1024)} %dynamic-update-slice, ...), channel_id=1, replica_groups=mesh['dp'=8,'tensor'=4] {'dp','tensor'}, use_global_device_ids=true, to_apply=%add.2 | all-reduce | flops 3840 | bytes 30720
  317.8 8.1 reduce-scatter.24.cloned.1.call-done
  332.2 26.1 %all-gather.2 = bf16[8,16,6]{1,2,0:T(8,128)(2,1)S(1)} all-gather(bf16[1,16,6]{1,2,0:T(8,128)(2,1)} %bitcast.318), channel_id=1, replica_groups=mesh['dp'=8,'tensor'=4] {'dp'}, dimensions={0}, use_global_device_ids=true | all-gather | bytes 1728 | tf_op jit(solution)/shard_map/all_gather | solution.py:181
  360.4 17.5 %all-gather.12.cloned.1.call-done = bf16[4096,768]{1,0:T(8,128)(2,1)} async-done(((bf16[1024,768]{1,0:T(8,128)(2,1)}), bf16[4096,768]{1,0:T(8,128)(2,1)}) %all-gather.12.cloned.1.call-update) | async-done | bytes 6291472 | tf_op jit(solution)/shard_map/all_gather | solution.py:226
  377.9 12.1 multiply_convert_fusion.2
  390.0 31.7 %all-gather.16.cloned.1.call-done = bf16[768,768]{0,1:T(8,128)(2,1)} async-done(((bf16[768,96]{0,1:T(8,128)(2,1)}), bf16[768,768]{0,1:T(8,128)(2,1)}) %all-gather.16.cloned.1.call-update) | async-done | bytes 1179664 | tf_op jit(solution)/shard_map/all_gather | solution.py:178
  421.7 9.2 convolution_convert_fusion.2
  431.0 56.8 %reduce-scatter.26.cloned.1.call-done = bf16[1024,768]{1,0:T(8,128)(2,1)} async-done(((bf16[4096,768]{1,0:T(8,128)(2,1)}), bf16[1024,768]{1,0:T(8,128)(2,1)}) %reduce-scatter.26.cloned.1.call-update) | async-done | bytes 1572880 | tf_op jit(solution)/shard_map/reduce_scatter | solution.py:233
  498.6 46.5 %all-gather.18.cloned.1.call-done = bf16[4096,768]{1,0:T(8,128)(2,1)} async-done(((bf16[1024,768]{1,0:T(8,128)(2,1)}), bf16[4096,768]{1,0:T(8,128)(2,1)}) %all-gather.18.cloned.1.call-update) | async-done | bytes 6291472 | tf_op jit(solution)/shard_map/all_gather | solution.py:246
  545.1 13.0 convert_reduce_fusion
  560.7 7.1 convolution_convert_fusion.1
  567.9 58.3 %reduce-scatter.28.cloned.1.call-done = bf16[1024,768]{1,0:T(8,128)(2,1)} async-done(((bf16[4096,768]{1,0:T(8,128)(2,1)}), bf16[1024,768]{1,0:T(8,128)(2,1)}) %reduce-scatter.28.cloned.1.call-update) | async-done | bytes 1572880 | tf_op jit(solution)/shard_map/reduce_scatter | solution.py:258
  626.2 5.3 multiply_reduce_fusion.2
  636.2 45.0 %all-gather.20.cloned.1.call-done = bf16[4096,768]{1,0:T(8,128)(2,1)} async-done(((bf16[1024,768]{1,0:T(8,128)(2,1)}), bf16[4096,768]{1,0:T(8,128)(2,1)}) %all-gather.20.cloned.1.call-update) | async-done | bytes 6291472 | tf_op jit(solution)/shard_map/all_gather | solution.py:272
  694.5 154.3 %while.27 = (s32[]{:T(128)}, bf16[4,1024,3,64]{1,3,2,0:T(8,128)(2,1)}, bf16[4,1024,3,64]{1,3,2,0:T(8,128)(2,1)}, bf16[4,1024,3,64]{1,3,2,0:T(8,128)(2,1)S(1)}, b...) while((s32[]{:T(128)}, ...), condition=%wide.region_22.23_spmd, body=%wide.region_19.22_spmd.sunk | while | flops 2063660032 | bytes 151801680 | solution.py:136
  704.2 5.7 multiply_reduce_fusion.9
  709.9 5.3 multiply_reduce_fusion.10
  715.2 7.6 multiply_convert_fusion.4
  742.7 5.7 multiply_reduce_fusion.9
  748.4 5.3 multiply_reduce_fusion.10
  753.7 7.6 multiply_convert_fusion.4
  781.1 5.7 multiply_reduce_fusion.9
  792.1 7.6 multiply_convert_fusion.4
  819.5 5.7 multiply_reduce_fusion.9
  830.5 7.6 multiply_convert_fusion.4
  855.2 6.4 fusion.113
  865.2 7.8 fusion.112
  876.3 13.2 add_convert_fusion
  889.6 10.1 fusion.114
  899.7 10.1 fusion.115
  910.0 5.5 convolution_bitcast_fusion.3
  917.8 5.5 convolution_bitcast_fusion.2
  928.5 5.5 convolution_bitcast_fusion.1
  936.8 21.6 %all-reduce.16 = (f32[3,64]{1,0:T(4,128)S(1)}, f32[3,64]{1,0:T(4,128)S(1)}) all-reduce(f32[3,64]{1,0:T(4,128)S(1)} %convert_reduce_fusion.3, f32[3,64]{1,0:T(4,128)S(1)} %convert_reduce_fusion.2), channel_id=12, replica_groups=mesh['dp'=8,'tensor'=4] {'dp'}, use_global_device_ids=true, to_apply=%region_31.32.clone | all-reduce | flops 384 | bytes 3072
  961.3 37.0 %reduce-scatter.30.cloned.1.call-done = bf16[1024,768]{1,0:T(8,128)(2,1)} async-done(((bf16[4096,768]{1,0:T(8,128)(2,1)}), bf16[1024,768]{1,0:T(8,128)(2,1)}) %reduce-scatter.30.cloned.1.call-update) | async-done | bytes 1572880 | tf_op jit(solution)/shard_map/reduce_scatter | solution.py:297
  1002.5 40.5 %all-reduce.14 = (f32[768]{0:T(1024)S(1)}, f32[768]{0:T(1024)S(1)}, f32[768]{0:T(1024)S(1)}, f32[768]{0:T(1024)S(1)}, f32[768]{0:T(1024)S(1)}, /*index=5*/f32[768]{0:T(1024)S(1)}, f32[768]{0:T(1024)S(1)}) all-reduce(f32[768]{0:T(1024)S(1)} %dynamic-update-slice.5, ...), channel_id=1, replica_groups=mesh['dp'=8,'tensor'=4] {'dp','tensor'}, use_global_device_ids=true, to_apply=%add.5 | all-reduce | flops 5376 | bytes 43008
  1048.2 24.0 %reduce-scatter.32.cloned.1.call-done = f32[96,768]{1,0:T(8,128)} async-done(((f32[768,768]{1,0:T(8,128)}), f32[96,768]{1,0:T(8,128)}) %reduce-scatter.32.cloned.1.call-update) | async-done | bytes 294928 | tf_op jit(solution)/shard_map/reduce_scatter | solution.py:315
  1072.2 72.5 %reduce-scatter.34.cloned.1.call-done = f32[768,96]{0,1:T(8,128)} async-done(((f32[768,768]{0,1:T(8,128)}), f32[768,96]{0,1:T(8,128)}) %reduce-scatter.34.cloned.1.call-update) | async-done | bytes 294928 | tf_op jit(solution)/shard_map/reduce_scatter | solution.py:316
  1144.7 65.8 %reduce-scatter.36.cloned.1.call-done = f32[96,192]{1,0:T(8,128)} async-done(((f32[768,192]{1,0:T(8,128)}), f32[96,192]{1,0:T(8,128)}) %reduce-scatter.36.cloned.1.call-update) | async-done | bytes 73744
  1210.5 65.5 %reduce-scatter.38.cloned.1.call-done = f32[96,192]{1,0:T(8,128)} async-done(((f32[768,192]{1,0:T(8,128)}), f32[96,192]{1,0:T(8,128)}) %reduce-scatter.38.cloned.1.call-update) | async-done | bytes 73744
  1276.0 65.7 %reduce-scatter.40.cloned.1.call-done = f32[96,192]{1,0:T(8,128)} async-done(((f32[768,192]{1,0:T(8,128)}), f32[96,192]{1,0:T(8,128)}) %reduce-scatter.40.cloned.1.call-update) | async-done | bytes 73744
  (379 shorter events, 266.1 us)
Async XLA Ops:
  8.0 140.5 %copy-start.38 = (bf16[96,192]{1,0:T(8,128)(2,1)S(1)}, bf16[96,192]{1,0:T(8,128)(2,1)}, u32[]{:S(2)}) copy-start(bf16[96,192]{1,0:T(8,128)(2,1)} %param.26) | copy-start | bytes 110596
  8.0 171.5 %all-gather.10.cloned.1.call-start = ((), (), s32[]{:S(2)}) async-start(), calls=%async_computation.11 | async-start | bytes 7864320 | tf_op jit(solution)/shard_map/all_gather | solution.py:204
  8.8 317.1 %reduce-scatter.24.cloned.1.call-start = ((), (), s32[]{:S(2)}) async-start(), calls=%async_computation.12 | async-start | bytes 7864320 | tf_op jit(solution)/shard_map/reduce_scatter | solution.py:218
  268.0 57.9 %copy-start.5 = (bf16[1024,768]{1,0:T(8,128)(2,1)S(1)}, bf16[1024,768]{1,0:T(8,128)(2,1)}, u32[]{:S(2)}) copy-start(bf16[1024,768]{1,0:T(8,128)(2,1)} %param.22) | copy-start | bytes 4718596
  268.0 92.4 %all-gather.14.cloned.1.call-start = ((), (), s32[]{:S(2)}) async-start(), calls=%async_computation.14 | async-start | bytes 1327104 | tf_op jit(solution)/shard_map/all_gather | solution.py:177
  268.6 109.3 %all-gather.12.cloned.1.call-start = ((), (), s32[]{:S(2)}) async-start(), calls=%async_computation.13 | async-start | bytes 7864320 | tf_op jit(solution)/shard_map/all_gather | solution.py:226
  331.6 90.1 %all-gather.16.cloned.1.call-start = ((), (), s32[]{:S(2)}) async-start(), calls=%async_computation.15 | async-start | bytes 1327104 | tf_op jit(solution)/shard_map/all_gather | solution.py:178
  332.2 155.6 %reduce-scatter.26.cloned.1.call-start = ((), (), s32[]{:S(2)}) async-start(), calls=%async_computation.16 | async-start | bytes 7864320 | tf_op jit(solution)/shard_map/reduce_scatter | solution.py:233
  430.9 114.1 %all-gather.18.cloned.1.call-start = ((), (), s32[]{:S(2)}) async-start(), calls=%async_computation.17 | async-start | bytes 7864320 | tf_op jit(solution)/shard_map/all_gather | solution.py:246
  490.8 4.9 copy-start.3
  490.9 4.8 copy-start.32
  491.4 7.1 copy-start.36
  498.5 127.6 %reduce-scatter.28.cloned.1.call-start = ((), (), s32[]{:S(2)}) async-start(), calls=%async_computation.18 | async-start | bytes 7864320 | tf_op jit(solution)/shard_map/reduce_scatter | solution.py:258
  545.1 15.6 %copy-start.48 = (bf16[768,768]{1,0:T(8,128)(2,1)S(1)}, bf16[768,768]{1,0:T(8,128)(2,1)}, u32[]{:S(2)}) copy-start(bf16[768,768]{1,0:T(8,128)(2,1)} %all-gather.14.cloned.1.call-done) | copy-start | bytes 3538948
  567.8 113.4 %all-gather.20.cloned.1.call-start = ((), (), s32[]{:S(2)}) async-start(), calls=%async_computation.19 | async-start | bytes 7864320 | tf_op jit(solution)/shard_map/all_gather | solution.py:272
  626.2 5.3 copy-start.7
  626.2 5.3 copy-start.9
  626.2 5.3 copy-start.18
  626.2 5.4 copy-start.27
  626.2 5.4 copy-start.29
  626.2 5.4 copy-start.31
  626.2 5.4 copy-start.35
  634.6 292.5 %reduce-scatter.44.cloned.1.call-start = ((), (), s32[]{:S(2)}) async-start(), calls=%async_computation.27 | async-start | bytes 73728
  636.1 323.6 %reduce-scatter.42.cloned.1.call-start = ((), (), s32[]{:S(2)}) async-start(), calls=%async_computation.26 | async-start | bytes 884736
  694.9 7.4 copy-start.1
  704.2 5.7 copy-start.11
  733.3 7.4 copy-start.1
  742.7 5.7 copy-start.11
  771.8 7.4 copy-start.1
  781.1 5.7 copy-start.11
  810.2 7.4 copy-start.1
  819.5 5.7 copy-start.11
  853.4 8.2 slice-start
  855.2 6.4 slice-start.1
  855.2 6.4 copy-start.15
  876.0 122.4 %reduce-scatter.30.cloned.1.call-start = ((), (), s32[]{:S(2)}) async-start(), calls=%async_computation.20 | async-start | bytes 7864320 | tf_op jit(solution)/shard_map/reduce_scatter | solution.py:297
  889.5 182.7 %reduce-scatter.32.cloned.1.call-start = ((), (), s32[]{:S(2)}) async-start(), calls=%async_computation.21 | async-start | bytes 2654208 | tf_op jit(solution)/shard_map/reduce_scatter | solution.py:315
  899.7 245.0 %reduce-scatter.34.cloned.1.call-start = ((), (), s32[]{:S(2)}) async-start(), calls=%async_computation.22 | async-start | bytes 2654208 | tf_op jit(solution)/shard_map/reduce_scatter | solution.py:316
  909.9 300.6 %reduce-scatter.36.cloned.1.call-start = ((), (), s32[]{:S(2)}) async-start(), calls=%async_computation.23 | async-start | bytes 884736
  917.7 7.9 copy-start.50
  917.7 9.1 copy-start.49
  917.7 358.3 %reduce-scatter.38.cloned.1.call-start = ((), (), s32[]{:S(2)}) async-start(), calls=%async_computation.24 | async-start | bytes 884736
  925.6 416.2 %reduce-scatter.40.cloned.1.call-start = ((), (), s32[]{:S(2)}) async-start(), calls=%async_computation.25 | async-start | bytes 884736
  998.4 4.1 copy-start.46
  998.4 48.1 %copy-start.4 = (f32[1024,768]{1,0:T(8,128)S(1)}, f32[1024,768]{1,0:T(8,128)}, u32[]{:S(2)}) copy-start(f32[1024,768]{1,0:T(8,128)} %copy-done.3) | copy-start | bytes 9437188
  998.4 48.1 %copy-start.33 = (f32[1024]{0:T(1024)S(1)}, f32[1024]{0:T(1024)}, u32[]{:S(2)}) copy-start(f32[1024]{0:T(1024)} %copy-done.32) | copy-start | bytes 12292
  998.4 48.1 %copy-start.37 = (f32[1024]{0:T(1024)S(1)}, f32[1024]{0:T(1024)}, u32[]{:S(2)}) copy-start(f32[1024]{0:T(1024)} %copy-done.36) | copy-start | bytes 12292
  998.4 48.1 %copy-start.40 = (f32[768]{0:T(1024)S(1)}, f32[768]{0:T(1024)}, u32[]{:S(2)}) copy-start(f32[768]{0:T(1024)} %get-tuple-element.338) | copy-start | bytes 9220
  (44 other events, 120.5 us)
Sparse Core Ops, SparseCore 0:
  10.4 49.0 all-gather.9
  268.1 57.7 reduce-scatter.23
  498.6 46.3 all-gather.17
  634.8 46.3 all-gather.19
Sparse Core Ops, SparseCore 1:
  270.9 39.8 all-gather.13
  331.7 46.1 all-gather.11
  380.2 41.5 all-gather.15
  431.0 56.7 reduce-scatter.25
  567.9 58.2 reduce-scatter.27
  639.8 61.4 reduce-scatter.43
  876.1 62.5 reduce-scatter.41
  941.1 57.2 reduce-scatter.29
  1002.7 69.4 reduce-scatter.31
  1076.7 68.0 reduce-scatter.33
  1148.8 61.6 reduce-scatter.35
  1214.4 61.6 reduce-scatter.37
  1280.1 61.5 reduce-scatter.39
where the time goes:
time: 1360 us; the launch traced here: 1350 us
  waiting for transfers between devices  596 us (44%)
  blocking collectives  295 us (22%)
  matrix products  276 us (20%)
  other arithmetic  88.6 us (7%)
  local copies, waits for them, and re-layouts  73.7 us (5%)
  between operations  17.1 us (1%)
    unnamed x22, waiting for transfers between devices  199 us
    unnamed x3, blocking collectives  101 us
    reduce_scatter x1, waiting for transfers between devices, per_device(): lax.psum_scatter(grad_w_down, 'dp', scatter_dimension=1, tiled=True)  72.5 us
    reduce_scatter x1, waiting for transfers between devices, per_device(): lax.psum_scatter(jnp.einsum('tf,df->td', piece, full_up, preferred_elemen...  58.3 us
    reduce_scatter x1, waiting for transfers between devices, per_device(): lax.psum_scatter(jnp.dot(piece, full_down, preferred_element_type=jnp.flo...  56.8 us
    all_gather x1, waiting for transfers between devices, per_device(): lax.all_gather(grad_two.astype(jnp.bfloat16), 'tensor', axis=0, tiled=True)  46.5 us
    all_gather x1, waiting for transfers between devices, per_device(): lax.all_gather(grad_one.astype(jnp.bfloat16), 'tensor', axis=0, tiled=True)  45 us
    dot_general x8, matrix products, one_sequence(): jnp.einsum('qhd,khd->hqk', grad_block, value_one, preferred_element_type=...  43.9 us
  transfers between devices with their start and end apart: 17, of which 13 were waited for; matrix products, arithmetic and copies ran while one was open for 22% of the time, Pallas kernels for 0%

commit v1 on v0

--- a/solution.py
+++ b/solution.py
@@ -9,6 +9,12 @@
 root_half = 0.7071067811865476
 inv_root_tau = 0.3989422804014327
 masked_value = -1e30
+
+
+def joined_along(pieces, dim):
+    pieces = jnp.moveaxis(pieces, 0, dim)
+    shape = pieces.shape
+    return pieces.reshape(*shape[:dim], shape[dim] * shape[dim + 1], *shape[dim + 2 :])
 
 
 def normalize(values, norm_gain, norm_shift):
@@ -243,7 +249,20 @@
     grad_gain_two = jnp.sum(grad_out * unit_two, axis=0)
     grad_shift_two = jnp.sum(grad_out, axis=0)
     grad_bias_down = jnp.sum(grad_two, axis=0)
-    grad_two_all = lax.all_gather(grad_two.astype(jnp.bfloat16), "tensor", axis=0, tiled=True)
+    x = grad_two.astype(jnp.bfloat16)
+    size = lax.axis_size("tensor")
+    pairs = [(i, (i + 1) % size) for i in range(size)]
+    back = [(b, a) for a, b in pairs]
+    lower, upper = ([], [])
+    for turn in range(size - 1):
+        if turn % 2 == 0:
+            lower.append(lax.ppermute(lower[-1] if lower else x, "tensor", pairs))
+        else:
+            upper.append(lax.ppermute(upper[-1] if upper else x, "tensor", back))
+    blocks = jnp.stack([*lower[::-1], x, *upper])
+    shift = lax.axis_index("tensor") - len(lower)
+    blocks = blocks[(jnp.arange(size) - shift) % size]
+    grad_two_all = joined_along(blocks, 0)
     grad_w_down = jnp.einsum(
         "tf,td->fd", activated, grad_two_all, preferred_element_type=jnp.float32
     )

time: 1360 us -> 1380 us (1.015)
    ppermute x0 -> x3, waiting for transfers between devices: none -> 54.2 us  [the longest x2 54.2 us: per_device(): lower.append(lax.ppermute(lower[-1] if lower else x, 'tensor', pairs))]
    all_gather x1 -> x0, waiting for transfers between devices: 46.5 us -> none  [per_device(): lax.all_gather(grad_two.astype(jnp.bfloat16), 'tensor', axis=0, tiled=True)]
    unnamed x22 -> x21, waiting for transfers between devices: 199 us -> 199 us
  transfers between devices with their start and end apart: 17 -> 19, of which waited for: 13 -> 14; matrix products, arithmetic and copies ran while one was open for 22% -> 22% of each run, Pallas kernels for 0% -> 0%
where the time goes in v1:
time: 1380 us; the launch traced here: 1370 us
  waiting for transfers between devices  604 us (44%)
  blocking collectives  295 us (21%)
  matrix products  275 us (20%)
  other arithmetic  96.1 us (7%)
  local copies, waits for them, and re-layouts  80 us (6%)
  between operations  17.1 us (1%)
    unnamed x21, waiting for transfers between devices  199 us
    unnamed x3, blocking collectives  101 us
    reduce_scatter x1, waiting for transfers between devices, per_device(): lax.psum_scatter(grad_w_down, 'dp', scatter_dimension=1, tiled=True)  72.6 us
    reduce_scatter x1, waiting for transfers between devices, per_device(): lax.psum_scatter(jnp.einsum('tf,df->td', piece, full_up, preferred_elemen...  58.2 us
    reduce_scatter x1, waiting for transfers between devices, per_device(): lax.psum_scatter(jnp.dot(piece, full_down, preferred_element_type=jnp.flo...  56.8 us
    ppermute x2, waiting for transfers between devices, per_device(): lower.append(lax.ppermute(lower[-1] if lower else x, 'tensor', pairs))  54.2 us
    all_gather x1, waiting for transfers between devices, per_device(): lax.all_gather(grad_one.astype(jnp.bfloat16), 'tensor', axis=0, tiled=True)  44.8 us
    dot_general x8, matrix products, one_sequence(): jnp.einsum('qhd,khd->hqk', grad_block, value_one, preferred_element_type=...  44 us
  transfers between devices with their start and end apart: 19, of which 14 were waited for; matrix products, arithmetic and copies ran while one was open for 22% of the time, Pallas kernels for 0%

profile of v1, /device:TPU:0, one launch (start us, length us, event | category | flops | bytes accessed | tf_op | source)
XLA Modules:
  0.0 1372.2 jit_solution(13643082405039575554)
XLA Ops:
  9.7 22.5 %all-gather.1 = bf16[8,8,3]{1,2,0:T(4,128)(2,1)S(1)} all-gather(bf16[1,8,3]{1,2,0:T(4,128)(2,1)} %bitcast.328), channel_id=1, replica_groups=mesh['dp'=8,'tensor'=4] {'dp'}, dimensions={0}, use_global_device_ids=true | all-gather | bytes 432 | tf_op jit(solution)/shard_map/all_gather | solution.py:185
  32.9 16.6 %all-gather = bf16[8,8,3]{1,2,0:T(4,128)(2,1)S(1)} all-gather(bf16[1,8,3]{1,2,0:T(4,128)(2,1)} %bitcast.329), channel_id=1, replica_groups=mesh['dp'=8,'tensor'=4] {'dp'}, dimensions={0}, use_global_device_ids=true | all-gather | bytes 432 | tf_op jit(solution)/shard_map/all_gather | solution.py:186
  50.7 31.2 %all_gather.60 = bf16[192,768]{0,1:T(8,128)(2,1)S(1)} all-gather(bf16[192,96]{0,1:T(8,128)(2,1)S(1)} %copy.104), channel_id=1, replica_groups=mesh['dp'=8,'tensor'=4] {'dp'}, dimensions={1}, use_global_device_ids=true | all-gather | bytes 331776 | tf_op jit(solution)/shard_map/all_gather | solution.py:182
  81.9 33.3 %all_gather.57 = bf16[768,192]{1,0:T(8,128)(2,1)} all-gather(bf16[96,192]{1,0:T(8,128)(2,1)} %param.24), channel_id=1, replica_groups=mesh['dp'=8,'tensor'=4] {'dp'}, dimensions={0}, use_global_device_ids=true | all-gather | bytes 331776 | tf_op jit(solution)/shard_map/all_gather | solution.py:179
  115.2 33.3 %all_gather.59 = bf16[768,192]{1,0:T(8,128)(2,1)} all-gather(bf16[96,192]{1,0:T(8,128)(2,1)} %param.25), channel_id=1, replica_groups=mesh['dp'=8,'tensor'=4] {'dp'}, dimensions={0}, use_global_device_ids=true | all-gather | bytes 331776 | tf_op jit(solution)/shard_map/all_gather | solution.py:180
  148.6 31.0 %all_gather.55 = bf16[768,192]{1,0:T(8,128)(2,1)S(1)} all-gather(bf16[96,192]{1,0:T(8,128)(2,1)S(1)} %copy-done.38), channel_id=1, replica_groups=mesh['dp'=8,'tensor'=4] {'dp'}, dimensions={0}, use_global_device_ids=true | all-gather | bytes 331776 | tf_op jit(solution)/shard_map/all_gather | solution.py:181
  205.9 52.6 %while.26 = (s32[]{:T(128)}, bf16[4,1024,3,64]{1,3,2,0:T(8,128)(2,1)}, f32[4,3,1024]{2,1,0:T(4,128)}, bf16[4,1024,3,64]{1,3,2,0:T(8,128)(2,1)}, s32[4,1024]{1,0:...) while((s32[]{:T(128)}, ...), condition=%wide.region_7.8_spmd, body=%wide.region_2.7_spmd.sunk | while | flops 845086720 | bytes 51542704 | solution.py:85
  278.4 39.3 %all-reduce.15 = (f32[768]{0:T(1024)}, f32[768]{0:T(1024)}, f32[768]{0:T(1024)}, f32[768]{0:T(1024)}, f32[768]{0:T(1024)}) all-reduce(f32[768]{0:T(1024)} %dynamic-update-slice.2, f32[768]{0:T(1024)} %dynamic-update-slice.1, f32[768]{0:T(1024)} %dynamic-update-slice, ...), channel_id=1, replica_groups=mesh['dp'=8,'tensor'=4] {'dp','tensor'}, use_global_device_ids=true, to_apply=%add.2 | all-reduce | flops 3840 | bytes 30720
  317.7 8.2 reduce-scatter.24.cloned.1.call-done
  332.2 26.1 %all-gather.2 = bf16[8,16,6]{1,2,0:T(8,128)(2,1)S(1)} all-gather(bf16[1,16,6]{1,2,0:T(8,128)(2,1)} %bitcast.327), channel_id=1, replica_groups=mesh['dp'=8,'tensor'=4] {'dp'}, dimensions={0}, use_global_device_ids=true | all-gather | bytes 1728 | tf_op jit(solution)/shard_map/all_gather | solution.py:187
  360.4 17.5 %all-gather.11.cloned.1.call-done = bf16[4096,768]{1,0:T(8,128)(2,1)} async-done(((bf16[1024,768]{1,0:T(8,128)(2,1)}), bf16[4096,768]{1,0:T(8,128)(2,1)}) %all-gather.11.cloned.1.call-update) | async-done | bytes 6291472 | tf_op jit(solution)/shard_map/all_gather | solution.py:232
  377.8 12.1 multiply_convert_fusion.2
  389.9 31.7 %all-gather.15.cloned.1.call-done = bf16[768,768]{0,1:T(8,128)(2,1)} async-done(((bf16[768,96]{0,1:T(8,128)(2,1)}), bf16[768,768]{0,1:T(8,128)(2,1)}) %all-gather.15.cloned.1.call-update) | async-done | bytes 1179664 | tf_op jit(solution)/shard_map/all_gather | solution.py:184
  421.7 9.2 convolution_convert_fusion.2
  430.9 56.8 %reduce-scatter.26.cloned.1.call-done = bf16[1024,768]{1,0:T(8,128)(2,1)} async-done(((bf16[4096,768]{1,0:T(8,128)(2,1)}), bf16[1024,768]{1,0:T(8,128)(2,1)}) %reduce-scatter.26.cloned.1.call-update) | async-done | bytes 1572880 | tf_op jit(solution)/shard_map/reduce_scatter | solution.py:239
  500.2 34.7 %collective-permute-done = bf16[1024,768]{1,0:T(8,128)(2,1)} collective-permute-done((bf16[1024,768]{1,0:T(8,128)(2,1)}, bf16[1024,768]{1,0:T(8,128)(2,1)}, u32[]{:S(2)}, u32[]{:S(2)}) %collective-permute-start) | collective-permute-done | bytes 1572896 | tf_op jit(solution)/shard_map/ppermute | solution.py:259
  535.5 19.5 %collective-permute-done.1 = bf16[1024,768]{1,0:T(8,128)(2,1)} collective-permute-done((bf16[1024,768]{1,0:T(8,128)(2,1)}, bf16[1024,768]{1,0:T(8,128)(2,1)}, u32[]{:S(2)}, u32[]{:S(2)}) %collective-permute-start.1) | collective-permute-done | bytes 1572896 | tf_op jit(solution)/shard_map/ppermute | solution.py:259
  555.0 6.9 pad_maximum_fusion
  562.0 6.4 gather_fusion
  568.4 12.8 convert_reduce_fusion
  583.8 7.1 convolution_convert_fusion.1
  591.0 58.2 %reduce-scatter.28.cloned.1.call-done = bf16[1024,768]{1,0:T(8,128)(2,1)} async-done(((bf16[4096,768]{1,0:T(8,128)(2,1)}), bf16[1024,768]{1,0:T(8,128)(2,1)}) %reduce-scatter.28.cloned.1.call-update) | async-done | bytes 1572880 | tf_op jit(solution)/shard_map/reduce_scatter | solution.py:277
  659.3 44.8 %all-gather.17.cloned.1.call-done = bf16[4096,768]{1,0:T(8,128)(2,1)} async-done(((bf16[1024,768]{1,0:T(8,128)(2,1)}), bf16[4096,768]{1,0:T(8,128)(2,1)}) %all-gather.17.cloned.1.call-update) | async-done | bytes 6291472 | tf_op jit(solution)/shard_map/all_gather | solution.py:291
  717.3 154.3 %while.27 = (s32[]{:T(128)}, bf16[4,1024,3,64]{1,3,2,0:T(8,128)(2,1)}, bf16[4,1024,3,64]{1,3,2,0:T(8,128)(2,1)}, bf16[4,1024,3,64]{1,3,2,0:T(8,128)(2,1)S(1)}, b...) while((s32[]{:T(128)}, ...), condition=%wide.region_22.23_spmd, body=%wide.region_19.22_spmd.sunk | while | flops 2063660032 | bytes 151801680 | solution.py:142
  727.0 5.7 multiply_reduce_fusion.9
  738.0 7.6 multiply_convert_fusion.4
  765.5 5.7 multiply_reduce_fusion.9
  776.5 7.6 multiply_convert_fusion.4
  803.9 5.7 multiply_reduce_fusion.9
  814.9 7.6 multiply_convert_fusion.4
  842.4 5.7 multiply_reduce_fusion.9
  853.4 7.6 multiply_convert_fusion.4
  878.0 6.4 fusion.115
  888.1 7.8 fusion.114
  899.1 13.2 add_convert_fusion
  912.4 10.1 fusion.116
  922.6 10.1 fusion.117
  932.8 5.5 convolution_bitcast_fusion.3
  940.6 5.5 convolution_bitcast_fusion.2
  951.3 5.5 convolution_bitcast_fusion.1
  959.7 21.6 %all-reduce.16 = (f32[3,64]{1,0:T(4,128)S(1)}, f32[3,64]{1,0:T(4,128)S(1)}) all-reduce(f32[3,64]{1,0:T(4,128)S(1)} %convert_reduce_fusion.3, f32[3,64]{1,0:T(4,128)S(1)} %convert_reduce_fusion.2), channel_id=12, replica_groups=mesh['dp'=8,'tensor'=4] {'dp'}, use_global_device_ids=true, to_apply=%region_31.32.clone | all-reduce | flops 384 | bytes 3072
  984.2 37.0 %reduce-scatter.30.cloned.1.call-done = bf16[1024,768]{1,0:T(8,128)(2,1)} async-done(((bf16[4096,768]{1,0:T(8,128)(2,1)}), bf16[1024,768]{1,0:T(8,128)(2,1)}) %reduce-scatter.30.cloned.1.call-update) | async-done | bytes 1572880 | tf_op jit(solution)/shard_map/reduce_scatter | solution.py:316
  1025.4 40.5 %all-reduce.14 = (f32[768]{0:T(1024)S(1)}, f32[768]{0:T(1024)S(1)}, f32[768]{0:T(1024)S(1)}, f32[768]{0:T(1024)S(1)}, f32[768]{0:T(1024)S(1)}, /*index=5*/f32[768]{0:T(1024)S(1)}, f32[768]{0:T(1024)S(1)}) all-reduce(f32[768]{0:T(1024)S(1)} %dynamic-update-slice.5, ...), channel_id=1, replica_groups=mesh['dp'=8,'tensor'=4] {'dp','tensor'}, use_global_device_ids=true, to_apply=%add.5 | all-reduce | flops 5376 | bytes 43008
  1071.1 24.0 %reduce-scatter.32.cloned.1.call-done = f32[96,768]{1,0:T(8,128)} async-done(((f32[768,768]{1,0:T(8,128)}), f32[96,768]{1,0:T(8,128)}) %reduce-scatter.32.cloned.1.call-update) | async-done | bytes 294928 | tf_op jit(solution)/shard_map/reduce_scatter | solution.py:334
  1095.1 72.6 %reduce-scatter.34.cloned.1.call-done = f32[768,96]{0,1:T(8,128)} async-done(((f32[768,768]{0,1:T(8,128)}), f32[768,96]{0,1:T(8,128)}) %reduce-scatter.34.cloned.1.call-update) | async-done | bytes 294928 | tf_op jit(solution)/shard_map/reduce_scatter | solution.py:335
  1167.7 65.7 %reduce-scatter.36.cloned.1.call-done = f32[96,192]{1,0:T(8,128)} async-done(((f32[768,192]{1,0:T(8,128)}), f32[96,192]{1,0:T(8,128)}) %reduce-scatter.36.cloned.1.call-update) | async-done | bytes 73744
  1233.3 65.5 %reduce-scatter.38.cloned.1.call-done = f32[96,192]{1,0:T(8,128)} async-done(((f32[768,192]{1,0:T(8,128)}), f32[96,192]{1,0:T(8,128)}) %reduce-scatter.38.cloned.1.call-update) | async-done | bytes 73744
  1298.9 65.7 %reduce-scatter.40.cloned.1.call-done = f32[96,192]{1,0:T(8,128)} async-done(((f32[768,192]{1,0:T(8,128)}), f32[96,192]{1,0:T(8,128)}) %reduce-scatter.40.cloned.1.call-update) | async-done | bytes 73744
  (386 shorter events, 284.3 us)
Async XLA Ops:
  8.0 140.5 %copy-start.38 = (bf16[96,192]{1,0:T(8,128)(2,1)S(1)}, bf16[96,192]{1,0:T(8,128)(2,1)}, u32[]{:S(2)}) copy-start(bf16[96,192]{1,0:T(8,128)(2,1)} %param.26) | copy-start | bytes 110596
  8.0 171.5 %all-gather.9.cloned.1.call-start = ((), (), s32[]{:S(2)}) async-start(), calls=%async_computation.11 | async-start | bytes 7864320 | tf_op jit(solution)/shard_map/all_gather | solution.py:210
  8.8 317.1 %reduce-scatter.24.cloned.1.call-start = ((), (), s32[]{:S(2)}) async-start(), calls=%async_computation.12 | async-start | bytes 7864320 | tf_op jit(solution)/shard_map/reduce_scatter | solution.py:224
  267.9 57.9 %copy-start.5 = (bf16[1024,768]{1,0:T(8,128)(2,1)S(1)}, bf16[1024,768]{1,0:T(8,128)(2,1)}, u32[]{:S(2)}) copy-start(bf16[1024,768]{1,0:T(8,128)(2,1)} %param.22) | copy-start | bytes 4718596
  268.0 92.4 %all-gather.13.cloned.1.call-start = ((), (), s32[]{:S(2)}) async-start(), calls=%async_computation.14 | async-start | bytes 1327104 | tf_op jit(solution)/shard_map/all_gather | solution.py:183
  268.5 109.3 %all-gather.11.cloned.1.call-start = ((), (), s32[]{:S(2)}) async-start(), calls=%async_computation.13 | async-start | bytes 7864320 | tf_op jit(solution)/shard_map/all_gather | solution.py:232
  331.6 90.1 %all-gather.15.cloned.1.call-start = ((), (), s32[]{:S(2)}) async-start(), calls=%async_computation.15 | async-start | bytes 1327104 | tf_op jit(solution)/shard_map/all_gather | solution.py:184
  332.1 155.6 %reduce-scatter.26.cloned.1.call-start = ((), (), s32[]{:S(2)}) async-start(), calls=%async_computation.16 | async-start | bytes 7864320 | tf_op jit(solution)/shard_map/reduce_scatter | solution.py:239
  430.9 218.3 %reduce-scatter.28.cloned.1.call-start = ((), (), s32[]{:S(2)}) async-start(), calls=%async_computation.17 | async-start | bytes 7864320 | tf_op jit(solution)/shard_map/reduce_scatter | solution.py:277
  490.8 4.9 copy-start.3
  491.4 7.1 copy-start.36
  498.4 36.4 %collective-permute-start = (bf16[1024,768]{1,0:T(8,128)(2,1)}, bf16[1024,768]{1,0:T(8,128)(2,1)}, u32[]{:S(2)}, u32[]{:S(2)}) collective-permute-start(bf16[1024,768]{1,0:T(8,128)(2,1)} %get-tuple-element.343), channel_id=1, source_target_pairs={{0,1},{1,2},{2,3},{3,0},{4,5},{5,6},{6,7},{7,4},{8,9},{9,10},{10,1... | collective-permute-start | bytes 4718600 | tf_op jit(solution)/shard_map/ppermute | solution.py:259
  498.4 37.1 %collective-permute-start.2 = (bf16[1024,768]{1,0:T(8,128)(2,1)}, bf16[1024,768]{1,0:T(8,128)(2,1)}, u32[]{:S(2)}, u32[]{:S(2)}) collective-permute-start(bf16[1024,768]{1,0:T(8,128)(2,1)} %get-tuple-element.343), channel_id=1, source_target_pairs={{1,0},{2,1},{3,2},{0,3},{5,4},{6,5},{7,6},{4,7},{9,8},{10,9},{11,1... | collective-permute-start | bytes 4718600 | tf_op jit(solution)/shard_map/ppermute | solution.py:261
  534.9 20.2 %collective-permute-start.1 = (bf16[1024,768]{1,0:T(8,128)(2,1)}, bf16[1024,768]{1,0:T(8,128)(2,1)}, u32[]{:S(2)}, u32[]{:S(2)}) collective-permute-start(bf16[1024,768]{1,0:T(8,128)(2,1)} %collective-permute-done), channel_id=1, source_target_pairs={{0,1},{1,2},{2,3},{3,0},{4,5},{5,6},{6,7},{7,4},{8,9},{9,10},{10,1... | collective-permute-start | bytes 4718600 | tf_op jit(solution)/shard_map/ppermute | solution.py:259
  568.4 15.4 %copy-start.48 = (bf16[768,768]{1,0:T(8,128)(2,1)S(1)}, bf16[768,768]{1,0:T(8,128)(2,1)}, u32[]{:S(2)}) copy-start(bf16[768,768]{1,0:T(8,128)(2,1)} %all-gather.13.cloned.1.call-done) | copy-start | bytes 3538948
  590.9 113.1 %all-gather.17.cloned.1.call-start = ((), (), s32[]{:S(2)}) async-start(), calls=%async_computation.18 | async-start | bytes 7864320 | tf_op jit(solution)/shard_map/all_gather | solution.py:291
  649.2 5.3 copy-start.7
  649.2 5.3 copy-start.9
  649.2 5.3 copy-start.18
  649.2 5.4 copy-start.27
  649.2 5.4 copy-start.29
  649.2 5.4 copy-start.31
  649.2 5.4 copy-start.35
  657.7 292.3 %reduce-scatter.44.cloned.1.call-start = ((), (), s32[]{:S(2)}) async-start(), calls=%async_computation.26 | async-start | bytes 73728
  659.2 323.4 %reduce-scatter.42.cloned.1.call-start = ((), (), s32[]{:S(2)}) async-start(), calls=%async_computation.25 | async-start | bytes 884736
  717.7 7.4 copy-start.1
  727.0 5.7 copy-start.11
  756.2 7.4 copy-start.1
  765.5 5.7 copy-start.11
  794.6 7.4 copy-start.1
  803.9 5.7 copy-start.11
  833.0 7.4 copy-start.1
  842.4 5.7 copy-start.11
  876.2 8.2 slice-start
  878.0 6.4 slice-start.1
  878.0 6.4 copy-start.15
  898.8 122.4 %reduce-scatter.30.cloned.1.call-start = ((), (), s32[]{:S(2)}) async-start(), calls=%async_computation.19 | async-start | bytes 7864320 | tf_op jit(solution)/shard_map/reduce_scatter | solution.py:316
  912.3 182.8 %reduce-scatter.32.cloned.1.call-start = ((), (), s32[]{:S(2)}) async-start(), calls=%async_computation.20 | async-start | bytes 2654208 | tf_op jit(solution)/shard_map/reduce_scatter | solution.py:334
  922.5 245.1 %reduce-scatter.34.cloned.1.call-start = ((), (), s32[]{:S(2)}) async-start(), calls=%async_computation.21 | async-start | bytes 2654208 | tf_op jit(solution)/shard_map/reduce_scatter | solution.py:335
  932.7 300.6 %reduce-scatter.36.cloned.1.call-start = ((), (), s32[]{:S(2)}) async-start(), calls=%async_computation.22 | async-start | bytes 884736
  940.6 7.9 copy-start.50
  940.6 9.1 copy-start.49
  940.6 358.3 %reduce-scatter.38.cloned.1.call-start = ((), (), s32[]{:S(2)}) async-start(), calls=%async_computation.23 | async-start | bytes 884736
  948.4 416.2 %reduce-scatter.40.cloned.1.call-start = ((), (), s32[]{:S(2)}) async-start(), calls=%async_computation.24 | async-start | bytes 884736
  1021.2 48.1 %copy-start.4 = (f32[1024,768]{1,0:T(8,128)S(1)}, f32[1024,768]{1,0:T(8,128)}, u32[]{:S(2)}) copy-start(f32[1024,768]{1,0:T(8,128)} %copy-done.3) | copy-start | bytes 9437188
  1021.3 48.1 %copy-start.33 = (f32[1024]{0:T(1024)S(1)}, f32[1024]{0:T(1024)}, u32[]{:S(2)}) copy-start(f32[1024]{0:T(1024)} %copy-done.32) | copy-start | bytes 12292
  1021.3 48.1 %copy-start.37 = (f32[1024]{0:T(1024)S(1)}, f32[1024]{0:T(1024)}, u32[]{:S(2)}) copy-start(f32[1024]{0:T(1024)} %copy-done.36) | copy-start | bytes 12292
  1021.3 48.1 %copy-start.40 = (f32[768]{0:T(1024)S(1)}, f32[768]{0:T(1024)}, u32[]{:S(2)}) copy-start(f32[768]{0:T(1024)} %get-tuple-element.338) | copy-start | bytes 9220
  (46 other events, 129.4 us)
Sparse Core Ops, SparseCore 0:
  10.4 49.0 all-gather.8
  268.1 57.7 reduce-scatter.23
  591.0 58.1 reduce-scatter.27
Sparse Core Ops, SparseCore 1:
  270.9 39.8 all-gather.12
  331.6 46.1 all-gather.10
  380.1 41.5 all-gather.14
  431.0 56.7 reduce-scatter.25
  657.8 46.2 all-gather.16
  708.4 61.3 reduce-scatter.43
  898.9 62.6 reduce-scatter.41
  963.9 57.3 reduce-scatter.29
  1025.6 69.4 reduce-scatter.31
  1099.6 68.0 reduce-scatter.33
  1171.8 61.5 reduce-scatter.35
  1237.2 61.6 reduce-scatter.37
  1303.0 61.5 reduce-scatter.39
